TPU v7x, 32 devices: a whole 2x2x4 slice. The times are simulated.
32 devices in a mesh: dp: 2 (over core), expert: 16 (over z, y, x).
Axes of the slice: x: 2, y: 2, z: 4, core: 2. Of those that a mesh axis runs over, the one named last changes fastest.
Arguments:
- tokens: bfloat16 [4096, 2048], P(('dp', 'expert')), may hold values from -6 to 6
- grad_out: bfloat16 [4096, 2048], P(('dp', 'expert')), may hold values from -6 to 6
- expert_ids: int32 [4096, 4], P(('dp', 'expert')), may hold values from 0 to 15, all different within a row; in each aligned block of 128 rows (0 to 127, 128 to 255, ...) at most 40 rows name the same one
- gate_values: bfloat16 [4096, 4], P(('dp', 'expert')), may hold values from 0.019897461 to 0.796875
- weight_in: bfloat16 [16, 2, 1408, 2048], P('expert', None, 'dp'), may hold values from -0.125 to 0.125
- weight_down: bfloat16 [16, 1408, 2048], P('expert', 'dp'), may hold values from -0.15625 to 0.15625
Outputs:
- grad_tokens: bfloat16 [4096, 2048], P(('dp', 'expert'))
- grad_gates: bfloat16 [4096, 4], P(('dp', 'expert'))
- grad_weight_in: bfloat16 [16, 2, 1408, 2048], P('expert', None, 'dp')
- grad_weight_down: bfloat16 [16, 1408, 2048], P('expert', 'dp')
Inputs may be any that keep to these rules, and one draw needn't show every extreme that they name: `expert_ids`: each row names 4 different experts. Within each aligned block of 128 rows (the rows of one device) no expert is named by more than 40 rows, and in some block some expert is named by exactly 40 rows.
All inputs are finite; a program needn't handle non-finite values.
Results may differ from a plain program's by a relative error of at most 0.008.
Values may be sent and summed in bfloat16 or wider, within the bound.
A program may use at most 128 MiB of HBM per device.

v0:
```python
import jax
import jax.numpy as jnp
from jax import lax
from jax.sharding import PartitionSpec as P


def expert_grads(inputs_rows, dy_rows, gate_rows, proj_in, proj_down):
    hidden = proj_in.shape[1]
    stacked = proj_in.reshape(2 * hidden, proj_in.shape[2])
    projected = lax.dot_general(
        inputs_rows, stacked, (((1,), (1,)), ((), ())), preferred_element_type=jnp.float32
    )
    gate_part = projected[:, :hidden]
    up_part = projected[:, hidden:]
    sigmoid_gate = jax.nn.sigmoid(gate_part)
    silu_gate = gate_part * sigmoid_gate
    hidden_act = (silu_gate * up_part).astype(jnp.bfloat16)
    upstream = lax.dot_general(
        dy_rows, proj_down, (((1,), (1,)), ((), ())), preferred_element_type=jnp.float32
    )
    gate_grad = jnp.sum(upstream * hidden_act.astype(jnp.float32), axis=1)
    gate_scale = gate_rows.astype(jnp.float32)[:, None]
    scaled_dy = (gate_scale * dy_rows.astype(jnp.float32)).astype(jnp.bfloat16)
    grad_down = lax.dot_general(
        hidden_act, scaled_dy, (((0,), (0,)), ((), ())), preferred_element_type=jnp.float32
    )
    hidden_grad = gate_scale * upstream
    grad_gate_part = (
        hidden_grad * up_part * sigmoid_gate * (1.0 + gate_part * (1.0 - sigmoid_gate))
    ).astype(jnp.bfloat16)
    grad_up_part = (hidden_grad * silu_gate).astype(jnp.bfloat16)
    joined = jnp.concatenate([grad_gate_part, grad_up_part], axis=1)
    row_grads = jnp.dot(joined, stacked, preferred_element_type=jnp.float32)
    grad_in = lax.dot_general(
        joined, inputs_rows, (((0,), (0,)), ((), ())), preferred_element_type=jnp.float32
    )
    return (row_grads, gate_grad, grad_in.reshape(2, hidden, proj_in.shape[2]), grad_down)


def slot_places(expert_ids, experts, capacity):
    flat_ids = expert_ids.reshape(-1)
    onehot = (flat_ids[:, None] == jnp.arange(experts, dtype=jnp.int32)[None, :]).astype(jnp.int32)
    running = jnp.cumsum(onehot, axis=0) - 1
    position = jnp.sum(onehot * running, axis=1)
    return flat_ids * capacity + position


def body(tokens, grad_out, expert_ids, gate_values, weight_in, weight_down):
    experts = lax.axis_size("expert")
    tok_rows = tokens.shape[0]
    feature_count = tokens.shape[1]
    top_count = expert_ids.shape[1]
    capacity = tok_rows * top_count * 5 // (4 * experts)
    slot_count = experts * capacity
    slot_index = slot_places(expert_ids, experts, capacity)
    pair_count = tok_rows * top_count
    owner_pair = (
        jnp.full((slot_count,), pair_count, jnp.int32)
        .at[slot_index]
        .set(jnp.arange(pair_count, dtype=jnp.int32))
    )
    token_of = owner_pair // top_count
    pad_row = jnp.zeros((1, feature_count), jnp.bfloat16)
    send_inputs = jnp.concatenate([tokens, pad_row], axis=0)[token_of].reshape(
        experts, capacity, feature_count
    )
    send_dy = jnp.concatenate([grad_out, pad_row], axis=0)[token_of].reshape(
        experts, capacity, feature_count
    )
    send_gate = jnp.concatenate([gate_values.reshape(-1), jnp.zeros((1,), jnp.bfloat16)])[
        owner_pair
    ].reshape(experts, capacity)
    recv_inputs, recv_dy, recv_gate = (
        lax.all_to_all(send_inputs, "expert", split_axis=0, concat_axis=0, tiled=True),
        lax.all_to_all(send_dy, "expert", split_axis=0, concat_axis=0, tiled=True),
        lax.all_to_all(send_gate, "expert", split_axis=0, concat_axis=0, tiled=True),
    )
    full_in, full_down = (
        lax.all_gather(weight_in, "dp", axis=2, tiled=True),
        lax.all_gather(weight_down, "dp", axis=1, tiled=True),
    )
    row_grads, gate_grad, grad_in, grad_down = expert_grads(
        recv_inputs.reshape(slot_count, feature_count),
        recv_dy.reshape(slot_count, feature_count),
        recv_gate.reshape(slot_count),
        full_in[0],
        full_down[0],
    )
    grad_in, grad_down = (
        lax.psum_scatter(grad_in, "dp", scatter_dimension=1, tiled=True),
        lax.psum_scatter(grad_down, "dp", scatter_dimension=0, tiled=True),
    )
    back_rows, back_gate = (
        lax.all_to_all(
            row_grads.astype(jnp.bfloat16).reshape(experts, capacity, feature_count),
            "expert",
            split_axis=0,
            concat_axis=0,
            tiled=True,
        ),
        lax.all_to_all(
            gate_grad.astype(jnp.bfloat16).reshape(experts, capacity),
            "expert",
            split_axis=0,
            concat_axis=0,
            tiled=True,
        ),
    )
    picked = back_rows.reshape(slot_count, feature_count)[slot_index].reshape(
        tok_rows, top_count, feature_count
    )
    grad_tokens = jnp.sum(picked, axis=1, dtype=jnp.float32).astype(jnp.bfloat16)
    grad_gates = back_gate.reshape(slot_count)[slot_index].reshape(tok_rows, top_count)
    return (
        grad_tokens,
        grad_gates,
        grad_in.astype(jnp.bfloat16)[None],
        grad_down.astype(jnp.bfloat16)[None],
    )


def solution(mesh):
    placed = (
        P(("dp", "expert"), None),
        P(("dp", "expert"), None),
        P(("dp", "expert"), None),
        P(("dp", "expert"), None),
        P("expert", None, "dp", None),
        P("expert", "dp", None),
    )
    return jax.shard_map(
        body,
        mesh=mesh,
        in_specs=placed,
        out_specs=(
            P(("dp", "expert"), None),
            P(("dp", "expert"), None),
            P("expert", None, "dp", None),
            P("expert", "dp", None),
        ),
        check_vma=False,
    )
```

profile of v0, /device:TPU:12, one launch (start us, length us, event | category | flops | bytes accessed | tf_op | source)
XLA Modules:
  0.0 318.7 jit_solution(16413516991251456437)
XLA Ops:
  12.8 4.3 %gather_fusion = bf16[640]{0:T(1024)(128)(2,1)S(1)} fusion(bf16[513]{0:T(1024)(128)(2,1)S(1)} %pad_maximum_fusion.2, s32[1024]{0:T(1024)S(1)} %get-tuple-element.21), kind=kCustom, calls=%fused_computation | custom fusion | bytes 5120 | tf_op jit(solution)/shard_map/gather | solution.py:70
  17.8 7.2 %all-to-all-start = ((bf16[16,1,40]{2,1,0:T(2,128)(2,1)}), bf16[16,1,40]{2,1,0:T(2,128)(2,1)S(1)}, u32[]{:S(2)}, u32[]{:S(2)}) async-start(bf16[16,1,40]{2,1,0:T(2,128)(2,1)} %all_to_all.25), calls=%async_computation | async-start | bytes 16384 | tf_op jit(solution)/shard_map/all_to_all | solution.py:76
  25.1 4.1 %gather_fusion.2 = bf16[640,2048]{1,0:T(8,128)(2,1)} fusion(bf16[129,2048]{1,0:T(8,128)(2,1)S(1)} %concatenate.14, s32[1024]{0:T(1024)S(1)} %get-tuple-element.20), kind=kCustom, calls=%fused_computation.2 | custom fusion | bytes 5245440 | tf_op jit(solution)/shard_map/gather | solution.py:64
  29.9 6.1 %all-to-all-start.2 = ((bf16[16,40,2048]{2,1,0:T(8,128)(2,1)}), bf16[16,40,2048]{2,1,0:T(8,128)(2,1)S(1)}, u32[]{:S(2)}, u32[]{:S(2)}) async-start(bf16[16,40,2048]{2,1,0:T(8,128)(2,1)} %bitcast.6), calls=%async_computation.2 | async-start | bytes 5242880 | tf_op jit(solution)/shard_map/all_to_all | solution.py:74
  37.9 4.1 %gather_fusion.1 = bf16[640,2048]{1,0:T(8,128)(2,1)} fusion(bf16[129,2048]{1,0:T(8,128)(2,1)S(1)} %concatenate.13, s32[1024]{0:T(1024)S(1)} %get-tuple-element.20), kind=kCustom, calls=%fused_computation.1 | custom fusion | bytes 5245440 | tf_op jit(solution)/shard_map/gather | solution.py:67
  41.9 53.0 %all-to-all-done.2 = bf16[16,40,2048]{2,1,0:T(8,128)(2,1)S(1)} async-done(((bf16[16,40,2048]{2,1,0:T(8,128)(2,1)}), bf16[16,40,2048]{2,1,0:T(8,128)(2,1)S(1)}, u32[]{:S(2)}, u32[]{:S(2)}) %all-to-all-start.2) | async-done | bytes 2621472 | tf_op jit(solution)/shard_map/all_to_all | solution.py:74
  94.9 4.8 %all-to-all-start.1 = ((bf16[16,40,2048]{2,1,0:T(8,128)(2,1)}), bf16[16,40,2048]{2,1,0:T(8,128)(2,1)}, u32[]{:S(2)}, u32[]{:S(2)}) async-start(bf16[16,40,2048]{2,1,0:T(8,128)(2,1)} %bitcast.3), calls=%async_computation.1 | async-start | bytes 5242880 | tf_op jit(solution)/shard_map/all_to_all | solution.py:75
  100.1 13.1 %fusion.14 = f32[640,2816]{1,0:T(8,128)} fusion(bf16[640,2048]{1,0:T(8,128)(2,1)S(1)} %bitcast.48, bf16[2816,2048]{1,0:T(8,128)(2,1)} %bitcast.54), kind=kOutput, calls=%fused_computation.49 | convolution fusion | flops 7381975040 | bytes 21364736 | tf_op jit(solution)/shard_map/dot_general | solution.py:10
  113.1 45.3 %all-to-all-done.1 = bf16[16,40,2048]{2,1,0:T(8,128)(2,1)} async-done(((bf16[16,40,2048]{2,1,0:T(8,128)(2,1)}), bf16[16,40,2048]{2,1,0:T(8,128)(2,1)}, u32[]{:S(2)}, u32[]{:S(2)}) %all-to-all-start.1) | async-done | bytes 2621472 | tf_op jit(solution)/shard_map/all_to_all | solution.py:75
  158.4 12.4 %multiply_reduce_fusion = (bf16[640]{0:T(1024)(128)(2,1)S(1)}, bf16[640,1408]{1,0:T(8,128)(2,1)S(1)}, bf16[640,1408]{1,0:T(8,128)(2,1)}, bf16[640,1408]{1,0:T(8,128)(2,1)}) fusion(f32[640,2816]{1,0:T(8,128)} %fusion.14, f32[640]{0:T(1024)S(1)} %reshape.128, bf16[640,2048]{1,0:T(8,128)(2,1)} %bitcast.4, bf16[1,1408,2048]{2,1,0:T(8,128)(2,1)} %all-gather.3.cloned.1.call-done), kind=kOutput, calls=%fused_computation.11 | convolution fusion | flops 3708108288 | bytes 21008128 | tf_op jit(solution)/shard_map/dot_general | solution.py:18
  170.8 9.5 %fusion.3 = f32[1408,2048]{1,0:T(8,128)} fusion(bf16[640,1408]{1,0:T(8,128)(2,1)S(1)} %get-tuple-element.13, bf16[640,2048]{1,0:T(8,128)(2,1)} %bitcast.4, f32[640]{0:T(1024)S(1)} %reshape.128), kind=kOutput, calls=%fused_computation.19 | convolution fusion | flops 3694919680 | bytes 15960576 | tf_op jit(solution)/shard_map/dot_general | solution.py:24
  180.7 4.1 %fusion.5 = bf16[2816,640]{0,1:T(8,128)(2,1)} fusion(bf16[640,1408]{1,0:T(8,128)(2,1)} %get-tuple-element.16, bf16[640,1408]{1,0:T(8,128)(2,1)} %get-tuple-element.17), kind=kLoop, calls=%fused_computation.21 | loop fusion | flops 7208960 | bytes 7208960 | tf_op jit(solution)/shard_map/dot_general | solution.py:34
  184.8 6.3 %copy.27 = bf16[2816,640]{1,0:T(8,128)(2,1)} copy(bf16[2816,640]{0,1:T(8,128)(2,1)} %fusion.5) | data formatting | bytes 7208960 | tf_op jit(solution)/shard_map/dot_general | solution.py:34
  191.0 15.1 %fusion.15 = f32[2,1408,2048]{2,1,0:T(8,128)} fusion(bf16[2,1408,640]{2,1,0:T(8,128)(2,1)} %bitcast.47, bf16[640,2048,1]{1,0,2:T(8,128)(2,1)S(1)} %bitcast.49), kind=kOutput, calls=%fused_computation.50 | convolution fusion | flops 7381975040 | bytes 29294592 | tf_op jit(solution)/shard_map/dot_general | solution.py:34
  206.9 5.3 %all-to-all-start.4 = ((bf16[16,1,40]{2,1,0:T(2,128)(2,1)}), bf16[16,1,40]{2,1,0:T(2,128)(2,1)S(1)}, u32[]{:S(2)}, u32[]{:S(2)}) async-start(bf16[16,1,40]{2,1,0:T(2,128)(2,1)} %convert_element_type.73), calls=%async_computation.4 | async-start | bytes 16384 | tf_op jit(solution)/shard_map/all_to_all | solution.py:101
  212.2 13.0 %convolution_convert_fusion = bf16[640,2048]{1,0:T(8,128)(2,1)} fusion(bf16[2816,2048]{1,0:T(8,128)(2,1)} %bitcast.55, bf16[640,1408]{1,0:T(8,128)(2,1)S(1)} %copy-done, bf16[640,1408]{1,0:T(8,128)(2,1)} %get-tuple-element.17), kind=kOutput, calls=%fused_computation.17 | convolution fusion | flops 7390494720 | bytes 17760256 | tf_op jit(solution)/shard_map/dot_general | solution.py:33
  225.2 6.9 %all-to-all-start.3 = ((bf16[16,40,2048]{2,1,0:T(8,128)(2,1)}), bf16[16,40,2048]{2,1,0:T(8,128)(2,1)S(1)}, u32[]{:S(2)}, u32[]{:S(2)}) async-start(bf16[16,40,2048]{2,1,0:T(8,128)(2,1)} %bitcast.50), calls=%async_computation.3 | async-start | bytes 5242880 | tf_op jit(solution)/shard_map/all_to_all | solution.py:94
  232.2 3.5 %gather_fusion.4 = bf16[512]{0:T(512)(128)(2,1)S(1)} fusion(bf16[640]{0:T(1024)(128)(2,1)S(1)} %reshape.126, s32[1024]{0:T(1024)S(1)} %pad_clamp_fusion), kind=kCustom, calls=%fused_computation.4 | custom fusion | bytes 4096 | tf_op jit(solution)/shard_map/gather | solution.py:113
  236.5 53.4 %all-to-all-done.3 = bf16[16,40,2048]{2,1,0:T(8,128)(2,1)S(1)} async-done(((bf16[16,40,2048]{2,1,0:T(8,128)(2,1)}), bf16[16,40,2048]{2,1,0:T(8,128)(2,1)S(1)}, u32[]{:S(2)}, u32[]{:S(2)}) %all-to-all-start.3) | async-done | bytes 2621472 | tf_op jit(solution)/shard_map/all_to_all | solution.py:94
  290.0 3.3 %gather_fusion.3 = bf16[512,2048]{1,0:T(8,128)(2,1)} fusion(bf16[640,2048]{1,0:T(8,128)(2,1)S(1)} %bitcast.46, s32[1024]{0:T(1024)S(1)} %pad_clamp_fusion), kind=kCustom, calls=%fused_computation.3 | custom fusion | bytes 4196352 | tf_op jit(solution)/shard_map/gather | solution.py:109
  293.2 2.7 reshape.125
  296.0 3.9 %reduce_sum.34 = bf16[128,2048]{1,0:T(8,128)(2,1)} reduce(bf16[128,4,2048]{2,1,0:T(4,128)(2,1)S(1)} %reshape.125, bf16[]{:T(256)} %constant.37.clone.1), dimensions={1}, to_apply=%region_4.5 | reduce | flops 786432 | bytes 2621442 | tf_op jit(solution)/shard_map/reduce_sum | solution.py:112
  299.8 4.7 %convert_bitcast_fusion.1 = bf16[1,704,2048]{2,1,0:T(8,128)(2,1)} fusion(f32[704,2048]{1,0:T(8,128)} %reduce-scatter.5.cloned.1.call-done), kind=kLoop, calls=%fused_computation.18 | loop fusion | flops 1441792 | bytes 8650752 | tf_op jit(solution)/shard_map/broadcast_in_dim | solution.py:118
  304.5 7.7 %convert_bitcast_fusion = bf16[1,2,704,2048]{3,2,1,0:T(8,128)(2,1)} fusion(f32[2,704,2048]{2,1,0:T(8,128)} %reduce-scatter.3.cloned.1.call-done), kind=kLoop, calls=%fused_computation.8 | loop fusion | flops 2883584 | bytes 17301504 | tf_op jit(solution)/shard_map/broadcast_in_dim | solution.py:117
  (53 shorter events, 11.2 us)
Async XLA Ops:
  7.2 0.8 copy-start.2
  7.2 1.1 copy-start.3
  7.2 17.8 %copy-start.1 = (bf16[128,2048]{1,0:T(8,128)(2,1)S(1)}, bf16[128,2048]{1,0:T(8,128)(2,1)}, u32[]{:S(2)}) copy-start(bf16[128,2048]{1,0:T(8,128)(2,1)} %param.6) | copy-start | bytes 1572868
  7.2 92.9 %all-gather.5.cloned.1.call-start = ((), (), s32[]{:S(2)}) async-start(), calls=%async_computation.8 | async-start | bytes 17301504 | tf_op jit(solution)/shard_map/all_gather | solution.py:79
  17.8 12.1 %all-to-all-start = ((bf16[16,1,40]{2,1,0:T(2,128)(2,1)}), bf16[16,1,40]{2,1,0:T(2,128)(2,1)S(1)}, u32[]{:S(2)}, u32[]{:S(2)}) async-start(bf16[16,1,40]{2,1,0:T(2,128)(2,1)} %all_to_all.25), calls=%async_computation | async-start | bytes 16384 | tf_op jit(solution)/shard_map/all_to_all | solution.py:76
  29.9 65.0 %all-to-all-start.2 = ((bf16[16,40,2048]{2,1,0:T(8,128)(2,1)}), bf16[16,40,2048]{2,1,0:T(8,128)(2,1)S(1)}, u32[]{:S(2)}, u32[]{:S(2)}) async-start(bf16[16,40,2048]{2,1,0:T(8,128)(2,1)} %bitcast.6), calls=%async_computation.2 | async-start | bytes 5242880 | tf_op jit(solution)/shard_map/all_to_all | solution.py:74
  36.0 122.4 %all-gather.3.cloned.1.call-start = ((), (), s32[]{:S(2)}) async-start(), calls=%async_computation.7 | async-start | bytes 8650752 | tf_op jit(solution)/shard_map/all_gather | solution.py:80
  94.9 63.5 %all-to-all-start.1 = ((bf16[16,40,2048]{2,1,0:T(8,128)(2,1)}), bf16[16,40,2048]{2,1,0:T(8,128)(2,1)}, u32[]{:S(2)}, u32[]{:S(2)}) async-start(bf16[16,40,2048]{2,1,0:T(8,128)(2,1)} %bitcast.3), calls=%async_computation.1 | async-start | bytes 5242880 | tf_op jit(solution)/shard_map/all_to_all | solution.py:75
  99.7 200.1 %reduce-scatter.5.cloned.1.call-start = ((), (), s32[]{:S(2)}) async-start(), calls=%async_computation.10 | async-start | bytes 17301504 | tf_op jit(solution)/shard_map/reduce_scatter | solution.py:91
  180.4 124.1 %reduce-scatter.3.cloned.1.call-start = ((), (), s32[]{:S(2)}) async-start(), calls=%async_computation.9 | async-start | bytes 34603008 | tf_op jit(solution)/shard_map/reduce_scatter | solution.py:90
  206.2 6.0 %copy-start = (bf16[640,1408]{1,0:T(8,128)(2,1)S(1)}, bf16[640,1408]{1,0:T(8,128)(2,1)}, u32[]{:S(2)}) copy-start(bf16[640,1408]{1,0:T(8,128)(2,1)} %get-tuple-element.16) | copy-start | bytes 5406724
  206.9 18.3 %all-to-all-start.4 = ((bf16[16,1,40]{2,1,0:T(2,128)(2,1)}), bf16[16,1,40]{2,1,0:T(2,128)(2,1)S(1)}, u32[]{:S(2)}, u32[]{:S(2)}) async-start(bf16[16,1,40]{2,1,0:T(2,128)(2,1)} %convert_element_type.73), calls=%async_computation.4 | async-start | bytes 16384 | tf_op jit(solution)/shard_map/all_to_all | solution.py:101
  225.2 64.8 %all-to-all-start.3 = ((bf16[16,40,2048]{2,1,0:T(8,128)(2,1)}), bf16[16,40,2048]{2,1,0:T(8,128)(2,1)S(1)}, u32[]{:S(2)}, u32[]{:S(2)}) async-start(bf16[16,40,2048]{2,1,0:T(8,128)(2,1)} %bitcast.50), calls=%async_computation.3 | async-start | bytes 5242880 | tf_op jit(solution)/shard_map/all_to_all | solution.py:94
Sparse Core Ops, SparseCore 0:
  9.6 24.4 all-gather.4
  38.4 17.1 all-gather.2
  180.5 19.2 reduce-scatter.4
  206.3 32.5 reduce-scatter.2
where the time goes:
time: 319 us
  waiting for transfers between devices  154 us (48%)
  matrix products  63.1 us (20%)
  local copies, waits for them, and re-layouts  35.2 us (11%)
  starting transfers between devices  30.8 us (10%)
  other arithmetic  21.7 us (7%)
  between operations  14 us (4%)
    all_to_all x1, waiting for transfers between devices, body(): lax.all_to_all(row_grads.astype(jnp.bfloat16).reshape(experts, capacity,...  53.4 us
    all_to_all x1, waiting for transfers between devices, body(): lax.all_to_all(send_inputs, 'expert', split_axis=0, concat_axis=0, tiled=...  53 us
    all_to_all x1, waiting for transfers between devices, body(): lax.all_to_all(send_dy, 'expert', split_axis=0, concat_axis=0, tiled=True)  45.3 us
    dot_general x1, matrix products, expert_grads(): lax.dot_general(joined, inputs_rows, (((0,), (0,)), ((), ())), preferred_...  15.1 us
    dot_general x1, matrix products, expert_grads(): lax.dot_general(inputs_rows, stacked, (((1,), (1,)), ((), ())), preferred...  13.1 us
    dot_general x1, matrix products, expert_grads(): row_grads = jnp.dot(joined, stacked, preferred_element_type=jnp.float32)  13 us
    dot_general x1, matrix products, expert_grads(): lax.dot_general(dy_rows, proj_down, (((1,), (1,)), ((), ())), preferred_e...  12.4 us
    dot_general x1, matrix products, expert_grads(): lax.dot_general(hidden_act, scaled_dy, (((0,), (0,)), ((), ())), preferre...  9.54 us
  transfers between devices with their start and end apart: 9, of which 4 were waited for; matrix products, arithmetic and copies ran while one was open for 28% of the time, Pallas kernels for 0%

commit v1 on v0

--- a/solution.py
+++ b/solution.py
@@ -2,6 +2,28 @@
 import jax.numpy as jnp
 from jax import lax
 from jax.sharding import PartitionSpec as P
+
+
+def cut_along(value, dim, count):
+    before, after = (value.shape[:dim], value.shape[dim + 1 :])
+    return jnp.moveaxis(value.reshape(*before, count, -1, *after), dim, 0)
+
+
+def in_order(blocks, dim):
+    blocks = jnp.moveaxis(blocks, 0, dim)
+    dims = blocks.shape
+    return blocks.reshape(*dims[:dim], dims[dim] * dims[dim + 1], *dims[dim + 2 :])
+
+
+def exchange_directly(shard, axis, split_dim, concat_dim):
+    size, place = (lax.axis_size(axis), lax.axis_index(axis))
+    pieces = cut_along(shard, split_dim, size)
+    finished = [pieces[place]]
+    for lap in range(1, size):
+        sent = pieces[(place + lap) % size]
+        finished.append(lax.ppermute(sent, axis, [(i, (i + lap) % size) for i in range(size)]))
+    pieces = jnp.stack(finished)[(place - jnp.arange(size)) % size]
+    return in_order(pieces, concat_dim)
 
 
 def expert_grads(inputs_rows, dy_rows, gate_rows, proj_in, proj_down):
@@ -71,7 +93,7 @@
         owner_pair
     ].reshape(experts, capacity)
     recv_inputs, recv_dy, recv_gate = (
-        lax.all_to_all(send_inputs, "expert", split_axis=0, concat_axis=0, tiled=True),
+        exchange_directly(send_inputs, "expert", 0, 0),
         lax.all_to_all(send_dy, "expert", split_axis=0, concat_axis=0, tiled=True),
         lax.all_to_all(send_gate, "expert", split_axis=0, concat_axis=0, tiled=True),
     )

time: 319 us -> 360 us (1.13)
  starting transfers between devices: 30.8 us -> 66.8 us
  local copies, waits for them, and re-layouts: 35.2 us -> 41.6 us
  waiting for transfers between devices: 154 us -> 150 us
    ppermute x0 -> x15, waiting for transfers between devices: none -> 106 us  [exchange_directly(): lax.ppermute(sent, axis, [(i, (i + lap) % size) for i in range(size)])]
    all_to_all x1 -> x0, waiting for transfers between devices: 53 us -> none  [body(): lax.all_to_all(send_inputs, 'expert', split_axis=0, concat_axis=0, tiled=...]
    all_to_all x1, waiting for transfers between devices: 45.3 us -> 0.01 us  [body(): lax.all_to_all(send_dy, 'expert', split_axis=0, concat_axis=0, tiled=True)]
    ppermute x0 -> x15, starting transfers between devices: none -> 34 us  [exchange_directly(): lax.ppermute(sent, axis, [(i, (i + lap) % size) for i in range(size)])]
    all_to_all x1, waiting for transfers between devices: 53.4 us -> 43.6 us  [body(): lax.all_to_all(row_grads.astype(jnp.bfloat16).reshape(experts, capacity,...]
    all_to_all x1, starting transfers between devices: 5.29 us -> 12.1 us  [body(): lax.all_to_all(gate_grad.astype(jnp.bfloat16).reshape(experts, capacity),...]
    all_to_all x1 -> x0, starting transfers between devices: 6.09 us -> none  [body(): lax.all_to_all(send_inputs, 'expert', split_axis=0, concat_axis=0, tiled=...]
    unnamed x11 -> x35, local copies, waits for them, and re-layouts: 0.92 us -> 4.85 us
  transfers between devices with their start and end apart: 9 -> 23, of which waited for: 4 -> 11; matrix products, arithmetic and copies ran while one was open for 28% -> 27% of each run, Pallas kernels for 0% -> 0%
where the time goes in v1:
time: 360 us
  waiting for transfers between devices  150 us (42%)
  starting transfers between devices  66.8 us (19%)
  matrix products  65.5 us (18%)
  local copies, waits for them, and re-layouts  41.6 us (12%)
  other arithmetic  21.2 us (6%)
  between operations  14.4 us (4%)
    ppermute x15, waiting for transfers between devices, exchange_directly(): lax.ppermute(sent, axis, [(i, (i + lap) % size) for i in range(size)])  106 us
    all_to_all x1, waiting for transfers between devices, body(): lax.all_to_all(row_grads.astype(jnp.bfloat16).reshape(experts, capacity,...  43.6 us
    ppermute x15, starting transfers between devices, exchange_directly(): lax.ppermute(sent, axis, [(i, (i + lap) % size) for i in range(size)])  34 us
    dot_general x1, matrix products, expert_grads(): lax.dot_general(joined, inputs_rows, (((0,), (0,)), ((), ())), preferred_...  16.6 us
    dot_general x1, matrix products, expert_grads(): lax.dot_general(inputs_rows, stacked, (((1,), (1,)), ((), ())), preferred...  13.8 us
    dot_general x1, matrix products, expert_grads(): row_grads = jnp.dot(joined, stacked, preferred_element_type=jnp.float32)  13 us
    all_to_all x1, starting transfers between devices, body(): lax.all_to_all(gate_grad.astype(jnp.bfloat16).reshape(experts, capacity),...  12.1 us
    dot_general x1, matrix products, expert_grads(): lax.dot_general(dy_rows, proj_down, (((1,), (1,)), ((), ())), preferred_e...  11.8 us
  transfers between devices with their start and end apart: 23, of which 11 were waited for; matrix products, arithmetic and copies ran while one was open for 27% of the time, Pallas kernels for 0%

profile of v1, /device:TPU:12, one launch (start us, length us, event | category | flops | bytes accessed | tf_op | source)
XLA Modules:
  0.0 359.7 jit_solution(15887712246620612888)
XLA Ops:
  17.8 7.2 %all-to-all-start = ((bf16[16,1,40]{2,1,0:T(2,128)(2,1)}), bf16[16,1,40]{2,1,0:T(2,128)(2,1)S(1)}, u32[]{:S(2)}, u32[]{:S(2)}) async-start(bf16[16,1,40]{2,1,0:T(2,128)(2,1)} %all_to_all.21), calls=%async_computation | async-start | bytes 16384 | tf_op jit(solution)/shard_map/all_to_all | solution.py:98
  42.5 6.3 %all-to-all-start.1 = ((bf16[16,40,2048]{2,1,0:T(8,128)(2,1)}), bf16[16,40,2048]{2,1,0:T(8,128)(2,1)}, u32[]{:S(2)}, u32[]{:S(2)}) async-start(bf16[16,40,2048]{2,1,0:T(8,128)(2,1)} %bitcast.3), calls=%async_computation.1 | async-start | bytes 5242880 | tf_op jit(solution)/shard_map/all_to_all | solution.py:97
  51.5 55.3 %collective-permute-done.1 = bf16[1,40,2048]{2,1,0:T(8,128)(2,1)S(1)} collective-permute-done((bf16[1,40,2048]{2,1,0:T(8,128)(2,1)}, bf16[1,40,2048]{2,1,0:T(8,128)(2,1)S(1)}, u32[]{:S(2)}, u32[]{:S(2)}) %collective-permute-start.1) | collective-permute-done | bytes 163872 | tf_op jit(solution)/shard_map/ppermute | solution.py:24
  106.8 5.3 %collective-permute-start.2 = (bf16[1,40,2048]{2,1,0:T(8,128)(2,1)}, bf16[1,40,2048]{2,1,0:T(8,128)(2,1)S(1)}, u32[]{:S(2)}, u32[]{:S(2)}) collective-permute-start(bf16[1,40,2048]{2,1,0:T(8,128)(2,1)} %get-tuple-element.30), channel_id=1, source_target_pairs={{0,3},{1,4},{2,5},{3,6},{4,7},{5,8},{6,9},{7,10},{8,11},{9,12},{10... | collective-permute-start | bytes 491528 | tf_op jit(solution)/shard_map/ppermute | solution.py:24
  116.0 6.4 %collective-permute-done.3 = bf16[1,40,2048]{2,1,0:T(8,128)(2,1)S(1)} collective-permute-done((bf16[1,40,2048]{2,1,0:T(8,128)(2,1)}, bf16[1,40,2048]{2,1,0:T(8,128)(2,1)S(1)}, u32[]{:S(2)}, u32[]{:S(2)}) %collective-permute-start.3) | collective-permute-done | bytes 163872 | tf_op jit(solution)/shard_map/ppermute | solution.py:24
  122.4 8.3 %collective-permute-done.4 = bf16[1,40,2048]{2,1,0:T(8,128)(2,1)S(1)} collective-permute-done((bf16[1,40,2048]{2,1,0:T(8,128)(2,1)}, bf16[1,40,2048]{2,1,0:T(8,128)(2,1)S(1)}, u32[]{:S(2)}, u32[]{:S(2)}) %collective-permute-start.4) | collective-permute-done | bytes 163872 | tf_op jit(solution)/shard_map/ppermute | solution.py:24
  130.7 5.7 %collective-permute-start.5 = (bf16[1,40,2048]{2,1,0:T(8,128)(2,1)}, bf16[1,40,2048]{2,1,0:T(8,128)(2,1)S(1)}, u32[]{:S(2)}, u32[]{:S(2)}) collective-permute-start(bf16[1,40,2048]{2,1,0:T(8,128)(2,1)} %get-tuple-element.27), channel_id=1, source_target_pairs={{0,6},{1,7},{2,8},{3,9},{4,10},{5,11},{6,12},{7,13},{8,14},{9,15},... | collective-permute-start | bytes 491528 | tf_op jit(solution)/shard_map/ppermute | solution.py:24
  140.3 4.4 %collective-permute-start.6 = (bf16[1,40,2048]{2,1,0:T(8,128)(2,1)}, bf16[1,40,2048]{2,1,0:T(8,128)(2,1)S(1)}, u32[]{:S(2)}, u32[]{:S(2)}) collective-permute-start(bf16[1,40,2048]{2,1,0:T(8,128)(2,1)} %get-tuple-element.26), channel_id=1, source_target_pairs={{0,7},{1,8},{2,9},{3,10},{4,11},{5,12},{6,13},{7,14},{8,15},{9,0},... | collective-permute-start | bytes 491528 | tf_op jit(solution)/shard_map/ppermute | solution.py:24
  144.7 4.4 %collective-permute-done.6 = bf16[1,40,2048]{2,1,0:T(8,128)(2,1)S(1)} collective-permute-done((bf16[1,40,2048]{2,1,0:T(8,128)(2,1)}, bf16[1,40,2048]{2,1,0:T(8,128)(2,1)S(1)}, u32[]{:S(2)}, u32[]{:S(2)}) %collective-permute-start.6) | collective-permute-done | bytes 163872 | tf_op jit(solution)/shard_map/ppermute | solution.py:24
  151.3 6.7 %collective-permute-done.7 = bf16[1,40,2048]{2,1,0:T(8,128)(2,1)S(1)} collective-permute-done((bf16[1,40,2048]{2,1,0:T(8,128)(2,1)}, bf16[1,40,2048]{2,1,0:T(8,128)(2,1)S(1)}, u32[]{:S(2)}, u32[]{:S(2)}) %collective-permute-start.7) | collective-permute-done | bytes 163872 | tf_op jit(solution)/shard_map/ppermute | solution.py:24
  158.0 8.3 %collective-permute-done.8 = bf16[1,40,2048]{2,1,0:T(8,128)(2,1)S(1)} collective-permute-done((bf16[1,40,2048]{2,1,0:T(8,128)(2,1)}, bf16[1,40,2048]{2,1,0:T(8,128)(2,1)S(1)}, u32[]{:S(2)}, u32[]{:S(2)}) %collective-permute-start.8) | collective-permute-done | bytes 163872 | tf_op jit(solution)/shard_map/ppermute | solution.py:24
  168.3 5.9 %collective-permute-done.9 = bf16[1,40,2048]{2,1,0:T(8,128)(2,1)S(1)} collective-permute-done((bf16[1,40,2048]{2,1,0:T(8,128)(2,1)S(1)}, bf16[1,40,2048]{2,1,0:T(8,128)(2,1)S(1)}, u32[]{:S(2)}, u32[]{:S(2)}) %collective-permute-start.9) | collective-permute-done | bytes 163872 | tf_op jit(solution)/shard_map/ppermute | solution.py:24
  174.2 4.7 %collective-permute-start.10 = (bf16[1,40,2048]{2,1,0:T(8,128)(2,1)S(1)}, bf16[1,40,2048]{2,1,0:T(8,128)(2,1)S(1)}, u32[]{:S(2)}, u32[]{:S(2)}) collective-permute-start(bf16[1,40,2048]{2,1,0:T(8,128)(2,1)S(1)} %get-tuple-element.22), channel_id=1, source_target_pairs={{0,11},{1,12},{2,13},{3,14},{4,15},{5,0},{6,1},{7,2},{8,3},{9,4},{... | collective-permute-start | bytes 491528 | tf_op jit(solution)/shard_map/ppermute | solution.py:24
  187.7 13.8 %fusion.16 = f32[640,2816]{1,0:T(8,128)} fusion(bf16[640,2048]{1,0:T(8,128)(2,1)} %bitcast.114, bf16[2816,2048]{1,0:T(8,128)(2,1)} %bitcast.119), kind=kOutput, calls=%fused_computation.88 | convolution fusion | flops 7381975040 | bytes 21364736 | tf_op jit(solution)/shard_map/dot_general | solution.py:32
  201.6 11.8 %multiply_reduce_fusion = (bf16[640]{0:T(1024)(128)(2,1)S(1)}, bf16[640,1408]{1,0:T(8,128)(2,1)S(1)}, bf16[640,1408]{1,0:T(8,128)(2,1)S(1)}, bf16[640,1408]{1,0:T(8,128)(2,1)}) fusion(f32[640,2816]{1,0:T(8,128)} %fusion.16, f32[640]{0:T(1024)S(1)} %reshape.169, bf16[640,2048]{1,0:T(8,128)(2,1)} %bitcast.4, ...), kind=kOutput, calls=%fused_computation.12 | convolution fusion | flops 3708108288 | bytes 21008128 | tf_op jit(solution)/shard_map/dot_general | solution.py:40
  213.4 10.2 %fusion.3 = f32[1408,2048]{1,0:T(8,128)} fusion(bf16[640,1408]{1,0:T(8,128)(2,1)S(1)} %get-tuple-element.13, bf16[640,2048]{1,0:T(8,128)(2,1)} %bitcast.4, f32[640]{0:T(1024)S(1)} %reshape.169), kind=kOutput, calls=%fused_computation.20 | convolution fusion | flops 3694919680 | bytes 15960576 | tf_op jit(solution)/shard_map/dot_general | solution.py:46
  227.4 6.0 %copy.27 = bf16[2816,640]{1,0:T(8,128)(2,1)} copy(bf16[2816,640]{0,1:T(8,128)(2,1)} %fusion.5) | data formatting | bytes 7208960 | tf_op jit(solution)/shard_map/dot_general | solution.py:56
  233.5 16.6 %fusion.17 = f32[2,1408,2048]{2,1,0:T(8,128)} fusion(bf16[2,1408,640]{2,1,0:T(8,128)(2,1)} %bitcast.111, bf16[640,2048,1]{1,0,2:T(8,128)(2,1)S(1)} %bitcast.115), kind=kOutput, calls=%fused_computation.89 | convolution fusion | flops 7381975040 | bytes 29294592 | tf_op jit(solution)/shard_map/dot_general | solution.py:56
  250.8 12.1 %all-to-all-start.3 = ((bf16[16,1,40]{2,1,0:T(2,128)(2,1)}), bf16[16,1,40]{2,1,0:T(2,128)(2,1)S(1)}, u32[]{:S(2)}, u32[]{:S(2)}) async-start(bf16[16,1,40]{2,1,0:T(2,128)(2,1)} %convert_element_type.73), calls=%async_computation.3 | async-start | bytes 16384 | tf_op jit(solution)/shard_map/all_to_all | solution.py:123
  262.9 13.0 %convolution_convert_fusion = bf16[640,2048]{1,0:T(8,128)(2,1)} fusion(bf16[2816,2048]{1,0:T(8,128)(2,1)} %bitcast.120, bf16[640,1408]{1,0:T(8,128)(2,1)S(1)} %copy-done.3, bf16[640,1408]{1,0:T(8,128)(2,1)} %get-tuple-element.17), kind=kOutput, calls=%fused_computation.18 | convolution fusion | flops 7390494720 | bytes 17760256 | tf_op jit(solution)/shard_map/dot_general | solution.py:55
  276.0 6.9 %all-to-all-start.2 = ((bf16[16,40,2048]{2,1,0:T(8,128)(2,1)}), bf16[16,40,2048]{2,1,0:T(8,128)(2,1)S(1)}, u32[]{:S(2)}, u32[]{:S(2)}) async-start(bf16[16,40,2048]{2,1,0:T(8,128)(2,1)} %bitcast.113), calls=%async_computation.2 | async-start | bytes 5242880 | tf_op jit(solution)/shard_map/all_to_all | solution.py:116
  287.3 43.6 %all-to-all-done.2 = bf16[16,40,2048]{2,1,0:T(8,128)(2,1)S(1)} async-done(((bf16[16,40,2048]{2,1,0:T(8,128)(2,1)}), bf16[16,40,2048]{2,1,0:T(8,128)(2,1)S(1)}, u32[]{:S(2)}, u32[]{:S(2)}) %all-to-all-start.2) | async-done | bytes 2621472 | tf_op jit(solution)/shard_map/all_to_all | solution.py:116
  340.8 4.7 %convert_bitcast_fusion.1 = bf16[1,704,2048]{2,1,0:T(8,128)(2,1)} fusion(f32[704,2048]{1,0:T(8,128)} %reduce-scatter.5.cloned.1.call-done), kind=kLoop, calls=%fused_computation.19 | loop fusion | flops 1441792 | bytes 8650752 | tf_op jit(solution)/shard_map/broadcast_in_dim | solution.py:140
  345.5 7.7 %convert_bitcast_fusion = bf16[1,2,704,2048]{3,2,1,0:T(8,128)(2,1)} fusion(f32[2,704,2048]{2,1,0:T(8,128)} %reduce-scatter.3.cloned.1.call-done), kind=kLoop, calls=%fused_computation.9 | loop fusion | flops 2883584 | bytes 17301504 | tf_op jit(solution)/shard_map/broadcast_in_dim | solution.py:139
  (110 shorter events, 69.9 us)
Async XLA Ops:
  7.2 180.6 %all-gather.5.cloned.1.call-start = ((), (), s32[]{:S(2)}) async-start(), calls=%async_computation.7 | async-start | bytes 17301504 | tf_op jit(solution)/shard_map/all_gather | solution.py:101
  17.8 24.6 %all-to-all-start = ((bf16[16,1,40]{2,1,0:T(2,128)(2,1)}), bf16[16,1,40]{2,1,0:T(2,128)(2,1)S(1)}, u32[]{:S(2)}, u32[]{:S(2)}) async-start(bf16[16,1,40]{2,1,0:T(2,128)(2,1)} %all_to_all.21), calls=%async_computation | async-start | bytes 16384 | tf_op jit(solution)/shard_map/all_to_all | solution.py:98
  25.0 176.6 %all-gather.3.cloned.1.call-start = ((), (), s32[]{:S(2)}) async-start(), calls=%async_computation.6 | async-start | bytes 8650752 | tf_op jit(solution)/shard_map/all_gather | solution.py:102
  30.1 154.5 %collective-permute-start.14 = (bf16[1,40,2048]{2,1,0:T(8,128)(2,1)S(1)}, bf16[1,40,2048]{2,1,0:T(8,128)(2,1)}, u32[]{:S(2)}, u32[]{:S(2)}) collective-permute-start(bf16[1,40,2048]{2,1,0:T(8,128)(2,1)S(1)} %get-tuple-element.18), channel_id=1, source_target_pairs={{0,15},{1,0},{2,1},{3,2},{4,3},{5,4},{6,5},{7,6},{8,7},{9,8},{10,9... | collective-permute-start | bytes 491528 | tf_op jit(solution)/shard_map/ppermute | solution.py:24
  31.5 152.1 %collective-permute-start.13 = (bf16[1,40,2048]{2,1,0:T(8,128)(2,1)S(1)}, bf16[1,40,2048]{2,1,0:T(8,128)(2,1)}, u32[]{:S(2)}, u32[]{:S(2)}) collective-permute-start(bf16[1,40,2048]{2,1,0:T(8,128)(2,1)S(1)} %get-tuple-element.19), channel_id=1, source_target_pairs={{0,14},{1,15},{2,0},{3,1},{4,2},{5,3},{6,4},{7,5},{8,6},{9,7},{10,... | collective-permute-start | bytes 491528 | tf_op jit(solution)/shard_map/ppermute | solution.py:24
  33.0 149.7 %collective-permute-start.12 = (bf16[1,40,2048]{2,1,0:T(8,128)(2,1)S(1)}, bf16[1,40,2048]{2,1,0:T(8,128)(2,1)}, u32[]{:S(2)}, u32[]{:S(2)}) collective-permute-start(bf16[1,40,2048]{2,1,0:T(8,128)(2,1)S(1)} %get-tuple-element.20), channel_id=1, source_target_pairs={{0,13},{1,14},{2,15},{3,0},{4,1},{5,2},{6,3},{7,4},{8,5},{9,6},{10... | collective-permute-start | bytes 491528 | tf_op jit(solution)/shard_map/ppermute | solution.py:24
  33.0 148.8 %collective-permute-start.11 = (bf16[1,40,2048]{2,1,0:T(8,128)(2,1)S(1)}, bf16[1,40,2048]{2,1,0:T(8,128)(2,1)}, u32[]{:S(2)}, u32[]{:S(2)}) collective-permute-start(bf16[1,40,2048]{2,1,0:T(8,128)(2,1)S(1)} %get-tuple-element.21), channel_id=1, source_target_pairs={{0,12},{1,13},{2,14},{3,15},{4,0},{5,1},{6,2},{7,3},{8,4},{9,5},{1... | collective-permute-start | bytes 491528 | tf_op jit(solution)/shard_map/ppermute | solution.py:24
  36.3 12.7 %collective-permute-start = (bf16[1,40,2048]{2,1,0:T(8,128)(2,1)}, bf16[1,40,2048]{2,1,0:T(8,128)(2,1)}, u32[]{:S(2)}, u32[]{:S(2)}) collective-permute-start(bf16[1,40,2048]{2,1,0:T(8,128)(2,1)} %get-tuple-element.32), channel_id=1, source_target_pairs={{0,1},{1,2},{2,3},{3,4},{4,5},{5,6},{6,7},{7,8},{8,9},{9,10},{10,1... | collective-permute-start | bytes 491528 | tf_op jit(solution)/shard_map/ppermute | solution.py:24
  42.5 159.1 %all-to-all-start.1 = ((bf16[16,40,2048]{2,1,0:T(8,128)(2,1)}), bf16[16,40,2048]{2,1,0:T(8,128)(2,1)}, u32[]{:S(2)}, u32[]{:S(2)}) async-start(bf16[16,40,2048]{2,1,0:T(8,128)(2,1)} %bitcast.3), calls=%async_computation.1 | async-start | bytes 5242880 | tf_op jit(solution)/shard_map/all_to_all | solution.py:97
  48.7 292.1 %reduce-scatter.5.cloned.1.call-start = ((), (), s32[]{:S(2)}) async-start(), calls=%async_computation.9 | async-start | bytes 17301504 | tf_op jit(solution)/shard_map/reduce_scatter | solution.py:113
  48.9 117.4 %copy-start.6 = (bf16[1,40,2048]{2,1,0:T(8,128)(2,1)S(1)}, bf16[1,40,2048]{2,1,0:T(8,128)(2,1)}, u32[]{:S(2)}) copy-start(bf16[1,40,2048]{2,1,0:T(8,128)(2,1)} %get-tuple-element.23) | copy-start | bytes 491524
  48.9 57.8 %collective-permute-start.1 = (bf16[1,40,2048]{2,1,0:T(8,128)(2,1)}, bf16[1,40,2048]{2,1,0:T(8,128)(2,1)S(1)}, u32[]{:S(2)}, u32[]{:S(2)}) collective-permute-start(bf16[1,40,2048]{2,1,0:T(8,128)(2,1)} %get-tuple-element.31), channel_id=1, source_target_pairs={{0,2},{1,3},{2,4},{3,5},{4,6},{5,7},{6,8},{7,9},{8,10},{9,11},{10,... | collective-permute-start | bytes 491528 | tf_op jit(solution)/shard_map/ppermute | solution.py:24
  106.8 9.2 %collective-permute-start.2 = (bf16[1,40,2048]{2,1,0:T(8,128)(2,1)}, bf16[1,40,2048]{2,1,0:T(8,128)(2,1)S(1)}, u32[]{:S(2)}, u32[]{:S(2)}) collective-permute-start(bf16[1,40,2048]{2,1,0:T(8,128)(2,1)} %get-tuple-element.30), channel_id=1, source_target_pairs={{0,3},{1,4},{2,5},{3,6},{4,7},{5,8},{6,9},{7,10},{8,11},{9,12},{10... | collective-permute-start | bytes 491528 | tf_op jit(solution)/shard_map/ppermute | solution.py:24
  116.0 6.4 %collective-permute-start.3 = (bf16[1,40,2048]{2,1,0:T(8,128)(2,1)}, bf16[1,40,2048]{2,1,0:T(8,128)(2,1)S(1)}, u32[]{:S(2)}, u32[]{:S(2)}) collective-permute-start(bf16[1,40,2048]{2,1,0:T(8,128)(2,1)} %get-tuple-element.29), channel_id=1, source_target_pairs={{0,4},{1,5},{2,6},{3,7},{4,8},{5,9},{6,10},{7,11},{8,12},{9,13},{1... | collective-permute-start | bytes 491528 | tf_op jit(solution)/shard_map/ppermute | solution.py:24
  122.4 8.3 %collective-permute-start.4 = (bf16[1,40,2048]{2,1,0:T(8,128)(2,1)}, bf16[1,40,2048]{2,1,0:T(8,128)(2,1)S(1)}, u32[]{:S(2)}, u32[]{:S(2)}) collective-permute-start(bf16[1,40,2048]{2,1,0:T(8,128)(2,1)} %get-tuple-element.28), channel_id=1, source_target_pairs={{0,5},{1,6},{2,7},{3,8},{4,9},{5,10},{6,11},{7,12},{8,13},{9,14},{... | collective-permute-start | bytes 491528 | tf_op jit(solution)/shard_map/ppermute | solution.py:24
  130.7 9.6 %collective-permute-start.5 = (bf16[1,40,2048]{2,1,0:T(8,128)(2,1)}, bf16[1,40,2048]{2,1,0:T(8,128)(2,1)S(1)}, u32[]{:S(2)}, u32[]{:S(2)}) collective-permute-start(bf16[1,40,2048]{2,1,0:T(8,128)(2,1)} %get-tuple-element.27), channel_id=1, source_target_pairs={{0,6},{1,7},{2,8},{3,9},{4,10},{5,11},{6,12},{7,13},{8,14},{9,15},... | collective-permute-start | bytes 491528 | tf_op jit(solution)/shard_map/ppermute | solution.py:24
  140.3 8.8 %collective-permute-start.6 = (bf16[1,40,2048]{2,1,0:T(8,128)(2,1)}, bf16[1,40,2048]{2,1,0:T(8,128)(2,1)S(1)}, u32[]{:S(2)}, u32[]{:S(2)}) collective-permute-start(bf16[1,40,2048]{2,1,0:T(8,128)(2,1)} %get-tuple-element.26), channel_id=1, source_target_pairs={{0,7},{1,8},{2,9},{3,10},{4,11},{5,12},{6,13},{7,14},{8,15},{9,0},... | collective-permute-start | bytes 491528 | tf_op jit(solution)/shard_map/ppermute | solution.py:24
  149.1 8.9 %collective-permute-start.7 = (bf16[1,40,2048]{2,1,0:T(8,128)(2,1)}, bf16[1,40,2048]{2,1,0:T(8,128)(2,1)S(1)}, u32[]{:S(2)}, u32[]{:S(2)}) collective-permute-start(bf16[1,40,2048]{2,1,0:T(8,128)(2,1)} %get-tuple-element.25), channel_id=1, source_target_pairs={{0,8},{1,9},{2,10},{3,11},{4,12},{5,13},{6,14},{7,15},{8,0},{9,1},... | collective-permute-start | bytes 491528 | tf_op jit(solution)/shard_map/ppermute | solution.py:24
  158.0 8.3 %collective-permute-start.8 = (bf16[1,40,2048]{2,1,0:T(8,128)(2,1)}, bf16[1,40,2048]{2,1,0:T(8,128)(2,1)S(1)}, u32[]{:S(2)}, u32[]{:S(2)}) collective-permute-start(bf16[1,40,2048]{2,1,0:T(8,128)(2,1)} %get-tuple-element.24), channel_id=1, source_target_pairs={{0,9},{1,10},{2,11},{3,12},{4,13},{5,14},{6,15},{7,0},{8,1},{9,2},... | collective-permute-start | bytes 491528 | tf_op jit(solution)/shard_map/ppermute | solution.py:24
  166.3 7.9 %collective-permute-start.9 = (bf16[1,40,2048]{2,1,0:T(8,128)(2,1)S(1)}, bf16[1,40,2048]{2,1,0:T(8,128)(2,1)S(1)}, u32[]{:S(2)}, u32[]{:S(2)}) collective-permute-start(bf16[1,40,2048]{2,1,0:T(8,128)(2,1)S(1)} %copy-done.6), channel_id=1, source_target_pairs={{0,10},{1,11},{2,12},{3,13},{4,14},{5,15},{6,0},{7,1},{8,2},{9,3},... | collective-permute-start | bytes 491528 | tf_op jit(solution)/shard_map/ppermute | solution.py:24
  174.2 7.6 %collective-permute-start.10 = (bf16[1,40,2048]{2,1,0:T(8,128)(2,1)S(1)}, bf16[1,40,2048]{2,1,0:T(8,128)(2,1)S(1)}, u32[]{:S(2)}, u32[]{:S(2)}) collective-permute-start(bf16[1,40,2048]{2,1,0:T(8,128)(2,1)S(1)} %get-tuple-element.22), channel_id=1, source_target_pairs={{0,11},{1,12},{2,13},{3,14},{4,15},{5,0},{6,1},{7,2},{8,3},{9,4},{... | collective-permute-start | bytes 491528 | tf_op jit(solution)/shard_map/ppermute | solution.py:24
  223.6 121.9 %reduce-scatter.3.cloned.1.call-start = ((), (), s32[]{:S(2)}) async-start(), calls=%async_computation.8 | async-start | bytes 34603008 | tf_op jit(solution)/shard_map/reduce_scatter | solution.py:112
  250.8 25.1 %all-to-all-start.3 = ((bf16[16,1,40]{2,1,0:T(2,128)(2,1)}), bf16[16,1,40]{2,1,0:T(2,128)(2,1)S(1)}, u32[]{:S(2)}, u32[]{:S(2)}) async-start(bf16[16,1,40]{2,1,0:T(2,128)(2,1)} %convert_element_type.73), calls=%async_computation.3 | async-start | bytes 16384 | tf_op jit(solution)/shard_map/all_to_all | solution.py:123
  276.0 55.0 %all-to-all-start.2 = ((bf16[16,40,2048]{2,1,0:T(8,128)(2,1)}), bf16[16,40,2048]{2,1,0:T(8,128)(2,1)S(1)}, u32[]{:S(2)}, u32[]{:S(2)}) async-start(bf16[16,40,2048]{2,1,0:T(8,128)(2,1)} %bitcast.113), calls=%async_computation.2 | async-start | bytes 5242880 | tf_op jit(solution)/shard_map/all_to_all | solution.py:116
  (8 other events, 64.8 us)
Sparse Core Ops, SparseCore 0:
  9.6 24.4 all-gather.4
  38.4 16.1 all-gather.2
  223.7 27.3 reduce-scatter.4
  253.2 36.3 reduce-scatter.2
